TPU v7x, 32 devices: a whole 2x2x4 slice. The times are simulated.
32 devices in a mesh: vol: 8 (over z, x), rep: 4 (over y, core).
Axes of the slice: x: 2, y: 2, z: 4, core: 2. Of those that a mesh axis runs over, the one named last changes fastest.
Arguments:
- cutouts: bfloat16 [4, 256, 4096], P('rep', 'vol'), may hold values from -6 to 6
- counts: int32 [4, 8], P('rep', 'vol'), may hold values from 1 to 32, as said below
- partner: int32 [4, 128], P('rep'), may hold values from 0 to 127, as said below
- w_stem: bfloat16 [64, 128], replicated, may hold values from -0.75 to 0.75
- w_mix: bfloat16 [128, 128], replicated, may hold values from -0.5 to 0.5
- w_out: bfloat16 [128, 128], replicated, may hold values from -0.5 to 0.5
- w_proj: bfloat16 [128, 64], replicated, may hold values from -0.5 to 0.5
Outputs:
- upd_stem: float32 [64, 128], replicated
- upd_mix: float32 [128, 128], replicated
- upd_out: float32 [128, 128], replicated
- upd_proj: float32 [128, 64], replicated
- node_loss: float32 [4, 8, 16], P('rep', 'vol')
Inputs may be any that keep to these rules, and one draw needn't show every extreme that they name: `counts`: each row sums to 128, and its largest entry is exactly 32. Each row pairs the nodes of a group: partner[r, partner[r, g]] = g and partner[r, g] != g.
All inputs are finite; a program needn't handle non-finite values.
Results may differ from a plain program's by a relative error of at most 0.0035.
Values may be sent and summed in bfloat16 or wider, within the bound.
No kernel may reach another device: no remote copies, remote signals or barrier semaphores. Data moves between devices by JAX's collectives and lax.ppermute only.
A program may use at most 64 MiB of HBM per device.

v0:
```python
import jax
import jax.numpy as jnp
from jax import lax
from jax.sharding import PartitionSpec as P

logit_divisor_factor = 0.2
norm_eps = 1e-06
rms_eps = 1e-06


def prefix(part, axis, combine, identity):
    place = lax.axis_index(axis)
    gathered = lax.all_gather(part, axis)
    state = jnp.zeros_like(part) + jnp.asarray(identity, part.dtype)

    def one(lap, state):
        return combine(state, lax.dynamic_index_in_dim(gathered, lap, 0, False))

    return lax.fori_loop(0, place, one, state)


def first_dot(left, right):
    return lax.dot_general(
        left, right, (((0,), (0,)), ((), ())), preferred_element_type=jnp.float32
    )


def concluding_matrix_multiply(left, right):
    return lax.dot_general(
        left, right, (((1,), (1,)), ((), ())), preferred_element_type=jnp.float32
    )


def silu_slope(value):
    sigma = jax.nn.sigmoid(value)
    return sigma * (1.0 + value * (1.0 - sigma))


def encode(cutout_rows, w_stem, w_mix, w_out, w_proj):
    number = cutout_rows.shape[0]
    patches = cutout_rows.reshape(-1, w_stem.shape[0])
    per_cutout = patches.shape[0] // number
    pre_stem = jnp.dot(patches, w_stem, preferred_element_type=jnp.float32)
    hidden = jax.nn.silu(pre_stem).astype(jnp.bfloat16)
    pre_mix = jnp.dot(hidden, w_mix, preferred_element_type=jnp.float32)
    mixed = jax.nn.silu(pre_mix).astype(jnp.bfloat16)
    summed = hidden.astype(jnp.float32) + jnp.dot(mixed, w_out, preferred_element_type=jnp.float32)
    pooled = jnp.mean(summed.reshape(number, per_cutout, -1), axis=1).astype(jnp.bfloat16)
    raw_embed = jnp.dot(pooled, w_proj, preferred_element_type=jnp.float32)
    inv_norm = lax.rsqrt(jnp.sum(raw_embed * raw_embed, axis=1, keepdims=True) + norm_eps)
    unit_embed = raw_embed * inv_norm
    return (unit_embed, (patches, pre_stem, hidden, pre_mix, mixed, pooled, unit_embed, inv_norm))


def backward(feature_vector_derivative, saved, w_mix, w_out, w_proj):
    patches, pre_stem, hidden, pre_mix, mixed, pooled, unit_embed, inv_norm = saved
    number = pooled.shape[0]
    per_cutout = patches.shape[0] // number
    channels = hidden.shape[1]
    radial = jnp.sum(unit_embed * feature_vector_derivative, axis=1, keepdims=True)
    grad_raw = (inv_norm * (feature_vector_derivative - unit_embed * radial)).astype(jnp.bfloat16)
    grad_proj = first_dot(pooled, grad_raw)
    grad_pool = (concluding_matrix_multiply(grad_raw, w_proj) / per_cutout).astype(jnp.bfloat16)
    mixed_sum = jnp.sum(mixed.reshape(number, per_cutout, channels), axis=1, dtype=jnp.float32)
    grad_out = lax.dot_general(
        mixed_sum,
        grad_pool.astype(jnp.float32),
        (((0,), (0,)), ((), ())),
        precision=lax.Precision.HIGHEST,
        preferred_element_type=jnp.float32,
    )
    grad_mixed = concluding_matrix_multiply(grad_pool, w_out)
    mix_slope = silu_slope(pre_mix).reshape(number, per_cutout, channels)
    grad_pre_mix = (grad_mixed[:, None, :] * mix_slope).reshape(-1, channels).astype(jnp.bfloat16)
    grad_mix = first_dot(hidden, grad_pre_mix)
    spread_pool = jnp.broadcast_to(
        grad_pool.astype(jnp.float32)[:, None, :], (number, per_cutout, channels)
    ).reshape(-1, channels)
    grad_hidden = spread_pool + concluding_matrix_multiply(grad_pre_mix, w_mix)
    grad_pre_stem = (grad_hidden * silu_slope(pre_stem)).astype(jnp.bfloat16)
    grad_stem = first_dot(patches, grad_pre_stem)
    return (grad_stem, grad_mix, grad_out, grad_proj)


def contrast(anchor_feature_matrix, whole_feature_matrix, self_pos, pair_pos):
    cosine_affinity_matrix = (
        concluding_matrix_multiply(anchor_feature_matrix, whole_feature_matrix)
        / logit_divisor_factor
    )
    columns = lax.broadcasted_iota(jnp.int32, cosine_affinity_matrix.shape, 1)
    exp_scores = jnp.where(columns == self_pos[:, None], 0.0, jnp.exp(cosine_affinity_matrix))
    log_total = jnp.log(jnp.sum(exp_scores, axis=1))
    companion_feature_vector = jnp.take(whole_feature_matrix, pair_pos, axis=0).astype(jnp.float32)
    positive_couple_affinity = (
        jnp.sum(anchor_feature_matrix.astype(jnp.float32) * companion_feature_vector, axis=1)
        / logit_divisor_factor
    )
    return (exp_scores, log_total, companion_feature_vector, log_total - positive_couple_affinity)


def add_counts(earlier, later):
    return earlier + later


def locate(recv_ids, node_rank, slot_index):
    matches = recv_ids[None, :] == node_rank[:, None]
    from_slot = jnp.sum(jnp.where(matches, slot_index[None, :], 0), axis=1)
    return (matches, from_slot)


def on_device(cutouts, counts, partner, w_stem, w_mix, w_out, w_proj):
    vol_size = lax.axis_size("vol")
    vol_index = lax.axis_index("vol")
    max_nodes = cutouts.shape[1]
    node_dev = partner.shape[1] // vol_size
    capacity = (max_nodes + vol_size - 1) // vol_size
    own_cutouts = cutouts[0]
    own_count = counts[0, 0]
    offset = prefix(counts, "vol", add_counts, jnp.zeros_like(counts))[0, 0]
    slot_index = jnp.arange(vol_size * capacity, dtype=jnp.int32)
    target = slot_index // capacity
    first_rank = (offset - target + vol_size - 1) // vol_size
    slot_rank = first_rank + slot_index % capacity
    local_slot = slot_rank * vol_size + target - offset
    is_live = local_slot < own_count
    local_safe = jnp.clip(local_slot, 0, max_nodes - 1)
    send_ids = jnp.where(is_live, slot_rank, -1).astype(jnp.int32)
    node_rank = jnp.arange(node_dev, dtype=jnp.int32)
    packed = jnp.where(
        is_live[:, None], jnp.take(own_cutouts, local_safe, axis=0), jnp.zeros((), jnp.bfloat16)
    )
    arrived, recv_ids = (
        lax.all_to_all(packed, "vol", split_axis=0, concat_axis=0, tiled=True),
        lax.all_to_all(send_ids, "vol", split_axis=0, concat_axis=0, tiled=True),
    )
    matches, from_slot = locate(recv_ids, node_rank, slot_index)
    unit_embed, saved = encode(jnp.take(arrived, from_slot, axis=0), w_stem, w_mix, w_out, w_proj)
    anchor_feature_matrix = unit_embed.astype(jnp.bfloat16)
    whole_feature_matrix = lax.all_gather(anchor_feature_matrix, "vol", axis=0, tiled=True)
    self_pos = vol_index * node_dev + node_rank
    node_global = node_rank * vol_size + vol_index
    pair_global = jnp.take(partner[0], node_global)
    pair_pos = pair_global % vol_size * node_dev + pair_global // vol_size
    exp_scores, log_total, companion_feature_vector, node_loss = contrast(
        anchor_feature_matrix, whole_feature_matrix, self_pos, pair_pos
    )
    row_weight = (exp_scores * jnp.exp(-log_total)[:, None]).astype(jnp.bfloat16)
    horizontal_objective_term = jnp.dot(
        row_weight, whole_feature_matrix, preferred_element_type=jnp.float32
    )
    all_totals = lax.all_gather(log_total, "vol", axis=0, tiled=True)
    column_weight = (exp_scores * jnp.exp(-all_totals)[None, :]).astype(jnp.bfloat16)
    vertical_objective_term = jnp.dot(
        column_weight, whole_feature_matrix, preferred_element_type=jnp.float32
    )
    feature_vector_derivative = (
        horizontal_objective_term + vertical_objective_term - 2.0 * companion_feature_vector
    ) / logit_divisor_factor
    grads = backward(feature_vector_derivative, saved, w_mix, w_out, w_proj)
    grad_totals = lax.psum((grads[0], grads[1], grads[2], grads[3]), ("vol", "rep"))
    updates = [
        summed_grad * lax.rsqrt(jnp.mean(summed_grad * summed_grad) + rms_eps)
        for summed_grad in grad_totals
    ]
    return (updates[0], updates[1], updates[2], updates[3], node_loss[None, None, :])


def solution(mesh):
    in_specs = (P("rep", "vol", None), P("rep", "vol"), P("rep", None), P(), P(), P(), P())
    out_specs = (P(), P(), P(), P(), P("rep", "vol", None))
    return jax.shard_map(
        on_device, mesh=mesh, in_specs=in_specs, out_specs=out_specs, check_vma=False
    )
```

profile of v0, /device:TPU:0, one launch (start us, length us, event | category | flops | bytes accessed | tf_op | source)
XLA Modules:
  0.0 372.9 jit_solution(8634578186639433932)
XLA Ops:
  7.9 0.6 dynamic-slice
  8.5 0.7 bitcast_dynamic-update-slice_fusion
  9.2 13.1 %all-reduce = s32[8]{0:T(128)S(1)} all-reduce(s32[8]{0:T(128)S(1)} %bitcast_dynamic-update-slice_fusion), channel_id=2, replica_groups=mesh['vol'=8,'rep'=4] {'vol'}, use_global_device_ids=true, to_apply=%add | all-reduce | flops 8 | bytes 64
  22.3 0.6 compare_select_fusion
  22.9 11.2 %all-to-all-start = ((s32[8,4,1]{1,2,0:T(1,128)}), s32[8,4,1]{1,2,0:T(1,128)S(1)}, u32[]{:S(2)}, u32[]{:S(2)}) async-start(s32[8,4,1]{1,2,0:T(1,128)} %compare_select_fusion), calls=%async_computation | async-start | bytes 8192 | tf_op jit(solution)/shard_map/all_to_all | solution.py:134
  34.2 0.6 copy-done.1
  34.8 0.7 gather_fusion.2
  35.6 0.7 gather_fusion
  36.5 0.9 select_select_fusion
  38.0 2.5 all-to-all-done
  40.6 3.5 all-to-all-start.1
  44.6 0.7 reduce.3
  45.7 6.6 %all-to-all-done.1 = bf16[8,4,4096]{2,1,0:T(4,128)(2,1)S(1)} async-done(((bf16[8,4,4096]{2,1,0:T(4,128)(2,1)}), bf16[8,4,4096]{2,1,0:T(4,128)(2,1)S(1)}, u32[]{:S(2)}, u32[]{:S(2)}) %all-to-all-start.1) | async-done | bytes 262176 | tf_op jit(solution)/shard_map/all_to_all | solution.py:133
  52.4 0.6 gather_fusion.1
  53.7 0.9 multiply_convert_fusion.1
  56.4 30.6 %all_gather.14 = bf16[128,64]{1,0:T(8,128)(2,1)S(1)} all-gather(bf16[16,64]{1,0:T(8,128)(2,1)S(1)} %multiply_convert_fusion.6), channel_id=1, replica_groups=mesh['vol'=8,'rep'=4] {'vol'}, dimensions={0}, use_global_device_ids=true | all-gather | bytes 18432 | tf_op jit(solution)/shard_map/all_gather | solution.py:139
  87.1 0.6 gather_fusion.3
  88.6 18.7 %all-reduce.1 = f32[128]{0:T(128)S(1)} all-reduce(f32[128]{0:T(128)S(1)} %get-tuple-element.60), channel_id=1, replica_groups=mesh['vol'=8,'rep'=4] {'vol'}, use_global_device_ids=true, to_apply=%add.1 | all-reduce | flops 128 | bytes 1024
  108.0 0.8 fusion.31
  109.2 0.9 fusion.51
  110.1 1.1 fusion.2
  111.3 0.9 fusion.52
  112.2 116.4 %all-reduce.7.cloned.1.call-done = (f32[64,128]{1,0:T(8,128)}, f32[128,64]{0,1:T(8,128)}) async-done(((f32[64,128]{1,0:T(8,128)}, f32[128,64]{0,1:T(8,128)}), (f32[64,128]{1,0:T(8,128)}, f32[128,64]{0,1:T(8,128)})) %all-reduce.7.cloned.1.call-update) | async-done | bytes 65552 | tf_op jit(solution)/shard_map/psum | solution.py:160
  228.6 1.4 multiply_reduce_fusion.2
  230.7 0.6 multiply_reduce_fusion.3
  232.0 0.6 broadcast_multiply_fusion.3
  232.8 0.6 broadcast_multiply_fusion.2
  233.4 127.7 %all-reduce.9.cloned.1.call-done = (f32[128,128]{1,0:T(8,128)}, f32[128,128]{1,0:T(8,128)}) async-done(((f32[128,128]{1,0:T(8,128)}, f32[128,128]{1,0:T(8,128)}), (f32[128,128]{1,0:T(8,128)}, f32[128,128]{1,0:T(8,128)})) %all-reduce.9.cloned.1.call-update) | async-done | bytes 131088 | tf_op jit(solution)/shard_map/psum | solution.py:160
  361.1 1.5 multiply_reduce_fusion
  363.3 0.6 multiply_reduce_fusion.1
  364.6 0.6 broadcast_multiply_fusion.1
  365.4 0.6 broadcast_multiply_fusion
  (64 shorter events, 6.1 us)
Async XLA Ops:
  7.2 28.5 %copy-start = (bf16[1,32,4096]{2,1,0:T(8,128)(2,1)S(1)}, bf16[1,32,4096]{2,1,0:T(8,128)(2,1)}, u32[]{:S(2)}) copy-start(bf16[1,32,4096]{2,1,0:T(8,128)(2,1)} %param.9) | copy-start | bytes 786436
  7.2 0.7 copy-start.10
  22.9 17.6 %all-to-all-start = ((s32[8,4,1]{1,2,0:T(1,128)}), s32[8,4,1]{1,2,0:T(1,128)S(1)}, u32[]{:S(2)}, u32[]{:S(2)}) async-start(s32[8,4,1]{1,2,0:T(1,128)} %compare_select_fusion), calls=%async_computation | async-start | bytes 8192 | tf_op jit(solution)/shard_map/all_to_all | solution.py:134
  34.2 0.7 copy-start.1
  40.6 11.7 %all-to-all-start.1 = ((bf16[8,4,4096]{2,1,0:T(4,128)(2,1)}), bf16[8,4,4096]{2,1,0:T(4,128)(2,1)S(1)}, u32[]{:S(2)}, u32[]{:S(2)}) async-start(bf16[8,4,4096]{2,1,0:T(4,128)(2,1)} %select_select_fusion), calls=%async_computation.1 | async-start | bytes 524288 | tf_op jit(solution)/shard_map/all_to_all | solution.py:133
  44.1 184.6 %all-reduce.7.cloned.1.call-start = ((), (), s32[]{:S(2)}) async-start(), calls=%async_computation.2 | async-start | bytes 131072 | tf_op jit(solution)/shard_map/psum | solution.py:160
  53.0 0.7 copy-start.9
  53.7 0.9 copy-start.8
  54.6 0.8 copy-start.7
  55.4 0.7 copy-start.6
  111.2 249.8 %all-reduce.9.cloned.1.call-start = ((), (), s32[]{:S(2)}) async-start(), calls=%async_computation.3 | async-start | bytes 262144 | tf_op jit(solution)/shard_map/psum | solution.py:160
  228.6 2.1 copy-start.5
  232.0 0.8 copy-start.4
  361.1 2.2 copy-start.3
  364.6 0.8 copy-start.2
Sparse Core Ops, SparseCore 0:
  111.4 117.2 all-reduce.6
  234.9 126.0 all-reduce.8
where the time goes:
time: 374 us; the launch traced here: 373 us
  waiting for transfers between devices  253 us (68%)
  blocking collectives  62.4 us (17%)
  between operations  18.4 us (5%)
  starting transfers between devices  14.8 us (4%)
  other arithmetic  10.2 us (3%)
  local copies, waits for them, and re-layouts  7.41 us (2%)
  matrix products  6.33 us (2%)
    psum x2, waiting for transfers between devices, on_device(): lax.psum((grads[0], grads[1], grads[2], grads[3]), ('vol', 'rep'))  244 us
    unnamed x2, blocking collectives  31.8 us
    all_gather x1, blocking collectives, on_device(): lax.all_gather(anchor_feature_matrix, 'vol', axis=0, tiled=True)  30.6 us
    all_to_all x1, starting transfers between devices, on_device(): lax.all_to_all(send_ids, 'vol', split_axis=0, concat_axis=0, tiled=True)  11.2 us
  transfers between devices with their start and end apart: 4, of which 4 were waited for; matrix products, arithmetic and copies ran while one was open for 2% of the time, Pallas kernels for 0%

commit v1 on v0

--- a/solution.py
+++ b/solution.py
@@ -157,7 +157,15 @@
         horizontal_objective_term + vertical_objective_term - 2.0 * companion_feature_vector
     ) / logit_divisor_factor
     grads = backward(feature_vector_derivative, saved, w_mix, w_out, w_proj)
-    grad_totals = lax.psum((grads[0], grads[1], grads[2], grads[3]), ("vol", "rep"))
+
+    def cut_fields(array_in):
+        which_axis = "vol"
+        axis_key = "rep"
+        for j in (which_axis, axis_key):
+            array_in = jax.lax.psum(array_in, j)
+        return array_in
+
+    grad_totals = cut_fields((grads[0], grads[1], grads[2], grads[3]))
     updates = [
         summed_grad * lax.rsqrt(jnp.mean(summed_grad * summed_grad) + rms_eps)
         for summed_grad in grad_totals

time: 374 us -> 332 us (0.89)
  waiting for transfers between devices: 253 us -> 211 us
    psum x2 -> x4, waiting for transfers between devices: 244 us -> 201 us  [cut_fields(): array_in = jax.lax.psum(array_in, j)]
  transfers between devices with their start and end apart: 4 -> 6, of which waited for: 4 -> 6; matrix products, arithmetic and copies ran while one was open for 2% -> 3% of each run, Pallas kernels for 0% -> 0%
where the time goes in v1:
time: 332 us; the launch traced here: 331 us
  waiting for transfers between devices  211 us (64%)
  blocking collectives  62.4 us (19%)
  between operations  18.2 us (5%)
  starting transfers between devices  14.9 us (4%)
  other arithmetic  10.2 us (3%)
  local copies, waits for them, and re-layouts  8.01 us (2%)
  matrix products  6.33 us (2%)
    psum x4, waiting for transfers between devices, cut_fields(): array_in = jax.lax.psum(array_in, j)  201 us
    unnamed x2, blocking collectives  31.8 us
    all_gather x1, blocking collectives, on_device(): lax.all_gather(anchor_feature_matrix, 'vol', axis=0, tiled=True)  30.6 us
    all_to_all x1, starting transfers between devices, on_device(): lax.all_to_all(send_ids, 'vol', split_axis=0, concat_axis=0, tiled=True)  11.2 us
  transfers between devices with their start and end apart: 6, of which 6 were waited for; matrix products, arithmetic and copies ran while one was open for 3% of the time, Pallas kernels for 0%

profile of v1, /device:TPU:0, one launch (start us, length us, event | category | flops | bytes accessed | tf_op | source)
XLA Modules:
  0.0 330.7 jit_solution(12899031979449577498)
XLA Ops:
  8.5 0.7 bitcast_dynamic-update-slice_fusion
  9.2 13.1 %all-reduce = s32[8]{0:T(128)S(1)} all-reduce(s32[8]{0:T(128)S(1)} %bitcast_dynamic-update-slice_fusion), channel_id=2, replica_groups=mesh['vol'=8,'rep'=4] {'vol'}, use_global_device_ids=true, to_apply=%add | all-reduce | flops 8 | bytes 64
  22.3 0.6 compare_select_fusion
  22.9 11.2 %all-to-all-start = ((s32[8,4,1]{1,2,0:T(1,128)}), s32[8,4,1]{1,2,0:T(1,128)S(1)}, u32[]{:S(2)}, u32[]{:S(2)}) async-start(s32[8,4,1]{1,2,0:T(1,128)} %compare_select_fusion), calls=%async_computation | async-start | bytes 8192 | tf_op jit(solution)/shard_map/all_to_all | solution.py:134
  34.2 0.6 copy-done.1
  34.8 0.7 gather_fusion.2
  35.6 0.7 gather_fusion
  36.5 0.9 select_select_fusion
  38.0 2.5 all-to-all-done
  40.6 3.5 %all-to-all-start.1 = ((bf16[8,4,4096]{2,1,0:T(4,128)(2,1)}), bf16[8,4,4096]{2,1,0:T(4,128)(2,1)S(1)}, u32[]{:S(2)}, u32[]{:S(2)}) async-start(bf16[8,4,4096]{2,1,0:T(4,128)(2,1)} %select_select_fusion), calls=%async_computation.1 | async-start | bytes 524288 | tf_op jit(solution)/shard_map/all_to_all | solution.py:133
  44.6 0.7 reduce.3
  45.7 6.6 %all-to-all-done.1 = bf16[8,4,4096]{2,1,0:T(4,128)(2,1)S(1)} async-done(((bf16[8,4,4096]{2,1,0:T(4,128)(2,1)}), bf16[8,4,4096]{2,1,0:T(4,128)(2,1)S(1)}, u32[]{:S(2)}, u32[]{:S(2)}) %all-to-all-start.1) | async-done | bytes 262176 | tf_op jit(solution)/shard_map/all_to_all | solution.py:133
  52.4 0.6 gather_fusion.1
  53.7 0.9 multiply_convert_fusion.1
  56.4 30.6 %all_gather.14 = bf16[128,64]{1,0:T(8,128)(2,1)S(1)} all-gather(bf16[16,64]{1,0:T(8,128)(2,1)S(1)} %multiply_convert_fusion.6), channel_id=1, replica_groups=mesh['vol'=8,'rep'=4] {'vol'}, dimensions={0}, use_global_device_ids=true | all-gather | bytes 18432 | tf_op jit(solution)/shard_map/all_gather | solution.py:139
  88.6 18.7 %all-reduce.1 = f32[128]{0:T(128)S(1)} all-reduce(f32[128]{0:T(128)S(1)} %get-tuple-element.64), channel_id=1, replica_groups=mesh['vol'=8,'rep'=4] {'vol'}, use_global_device_ids=true, to_apply=%add.1 | all-reduce | flops 128 | bytes 1024
  108.0 0.8 fusion.31
  109.2 1.1 fusion.2
  110.4 0.9 fusion.51
  111.3 66.0 %all-reduce.11.cloned.1.call-done = (f32[64,128]{1,0:T(8,128)}, f32[128,64]{0,1:T(8,128)}) async-done(((f32[64,128]{1,0:T(8,128)}, f32[128,64]{0,1:T(8,128)}), (f32[64,128]{1,0:T(8,128)}, f32[128,64]{0,1:T(8,128)})) %all-reduce.11.cloned.1.call-update) | async-done | bytes 65552 | tf_op jit(solution)/shard_map/psum | solution.py:165
  177.4 0.9 fusion.52
  178.3 32.9 %all-reduce.15.cloned.1.call-done = (f32[64,128]{1,0:T(8,128)}, f32[128,64]{0,1:T(8,128)}) async-done(((f32[64,128]{1,0:T(8,128)}, f32[128,64]{0,1:T(8,128)}), (f32[64,128]{1,0:T(8,128)}, f32[128,64]{0,1:T(8,128)})) %all-reduce.15.cloned.1.call-update) | async-done | bytes 65552 | tf_op jit(solution)/shard_map/psum | solution.py:165
  211.2 1.4 multiply_reduce_fusion.2
  214.6 0.6 broadcast_multiply_fusion.3
  215.2 70.8 %all-reduce.13.cloned.1.call-done = (f32[128,128]{1,0:T(8,128)}, f32[128,128]{1,0:T(8,128)}) async-done(((f32[128,128]{1,0:T(8,128)}, f32[128,128]{1,0:T(8,128)}), (f32[128,128]{1,0:T(8,128)}, f32[128,128]{1,0:T(8,128)})) %all-reduce.13.cloned.1.call-update) | async-done | bytes 131088 | tf_op jit(solution)/shard_map/psum | solution.py:165
  286.0 0.7 copy-done.4
  286.7 0.6 broadcast_multiply_fusion.2
  287.4 31.8 %all-reduce.17.cloned.1.call-done = (f32[128,128]{1,0:T(8,128)}, f32[128,128]{1,0:T(8,128)}) async-done(((f32[128,128]{1,0:T(8,128)}, f32[128,128]{1,0:T(8,128)}), (f32[128,128]{1,0:T(8,128)}, f32[128,128]{1,0:T(8,128)})) %all-reduce.17.cloned.1.call-update) | async-done | bytes 131088 | tf_op jit(solution)/shard_map/psum | solution.py:165
  319.2 1.5 multiply_reduce_fusion
  321.4 0.6 multiply_reduce_fusion.1
  322.7 0.6 broadcast_multiply_fusion.1
  323.5 0.6 broadcast_multiply_fusion
  (70 shorter events, 7.9 us)
Async XLA Ops:
  7.2 28.5 %copy-start = (bf16[1,32,4096]{2,1,0:T(8,128)(2,1)S(1)}, bf16[1,32,4096]{2,1,0:T(8,128)(2,1)}, u32[]{:S(2)}) copy-start(bf16[1,32,4096]{2,1,0:T(8,128)(2,1)} %param.9) | copy-start | bytes 786436
  7.2 0.7 copy-start.10
  22.9 17.6 %all-to-all-start = ((s32[8,4,1]{1,2,0:T(1,128)}), s32[8,4,1]{1,2,0:T(1,128)S(1)}, u32[]{:S(2)}, u32[]{:S(2)}) async-start(s32[8,4,1]{1,2,0:T(1,128)} %compare_select_fusion), calls=%async_computation | async-start | bytes 8192 | tf_op jit(solution)/shard_map/all_to_all | solution.py:134
  34.2 0.7 copy-start.1
  40.6 11.7 %all-to-all-start.1 = ((bf16[8,4,4096]{2,1,0:T(4,128)(2,1)}), bf16[8,4,4096]{2,1,0:T(4,128)(2,1)S(1)}, u32[]{:S(2)}, u32[]{:S(2)}) async-start(bf16[8,4,4096]{2,1,0:T(4,128)(2,1)} %select_select_fusion), calls=%async_computation.1 | async-start | bytes 524288 | tf_op jit(solution)/shard_map/all_to_all | solution.py:133
  44.1 133.2 %all-reduce.11.cloned.1.call-start = ((), (), s32[]{:S(2)}) async-start(), calls=%async_computation.2 | async-start | bytes 131072 | tf_op jit(solution)/shard_map/psum | solution.py:165
  53.0 0.7 copy-start.9
  53.7 0.9 copy-start.8
  54.6 0.8 copy-start.7
  55.4 0.7 copy-start.6
  110.3 100.9 %all-reduce.15.cloned.1.call-start = ((), (), s32[]{:S(2)}) async-start(), calls=%async_computation.4 | async-start | bytes 131072 | tf_op jit(solution)/shard_map/psum | solution.py:165
  177.3 108.7 %all-reduce.13.cloned.1.call-start = ((), (), s32[]{:S(2)}) async-start(), calls=%async_computation.3 | async-start | bytes 262144 | tf_op jit(solution)/shard_map/psum | solution.py:165
  178.3 140.9 %all-reduce.17.cloned.1.call-start = ((), (), s32[]{:S(2)}) async-start(), calls=%async_computation.5 | async-start | bytes 262144 | tf_op jit(solution)/shard_map/psum | solution.py:165
  211.2 2.1 copy-start.5
  286.0 0.8 copy-start.4
  319.2 2.2 copy-start.3
  322.7 0.8 copy-start.2
Sparse Core Ops, SparseCore 0:
  110.5 66.7 all-reduce.10
  179.7 31.4 all-reduce.14
  215.3 70.6 all-reduce.12
  288.2 30.9 all-reduce.16
